TPU v7x, 32 devices: a whole 2x2x4 slice. The times are simulated.
32 devices in a mesh: dap: 32 (over z, y, x, core).
Axes of the slice: x: 2, y: 2, z: 4, core: 2. Of those that a mesh axis runs over, the one named last changes fastest.
Arguments:
- homolog_stack: float32 [64, 64, 256], P('dap'), may hold values from -5 to 5
- couple_tensor: float32 [64, 64, 128], P('dap'), may hold values from -6 to 6
- homolog_presence: int32 [64, 64], P('dap'), may hold values from 0 to 1
- amino_presence: int32 [64], replicated, may hold values 0 or 1
- horizontal_standard_factor: float32 [256], replicated, may hold values from 0.5 to 1.5
- horizontal_asking_matrix: bfloat16 [256, 256], replicated, may hold values from -7 to 7
- horizontal_lookup_triple: bfloat16 [256, 768], replicated, may hold values from -0.375 to 0.375
- horizontal_final_matrix: bfloat16 [256, 256], replicated, may hold values from -0.375 to 0.375
- couple_offset_factor: float32 [128], replicated, may hold values from 0.5 to 1.5
- couple_offset_matrix: bfloat16 [128, 8], replicated, may hold values from -2 to 2
- vertical_standard_factor: float32 [256], replicated, may hold values from 0.5 to 1.5
- vertical_asking_matrix: bfloat16 [256, 256], replicated, may hold values from -7 to 7
- vertical_lookup_triple: bfloat16 [256, 768], replicated, may hold values from -0.375 to 0.375
- vertical_final_matrix: bfloat16 [256, 256], replicated, may hold values from -0.375 to 0.375
- tensor_average_factor: float32 [256], replicated, may hold values from 0.5 to 1.5
- tensor_average_mapping: bfloat16 [256, 64], replicated, may hold values from -0.375 to 0.375
- tensor_average_final: bfloat16 [1024, 128], replicated, may hold values from -0.375 to 0.375
- trio_entry_factors: float32 [2, 128], replicated, may hold values from 0.5 to 1.5
- trio_flank_mappings: bfloat16 [2, 128, 512], replicated, may hold values from -0.5 to 0.5
- trio_final_switches: bfloat16 [2, 128, 128], replicated, may hold values from -0.5 to 0.5
- trio_multiplied_factors: float32 [2, 128], replicated, may hold values from 0.5 to 1.5
- trio_final_matrices: bfloat16 [2, 128, 128], replicated, may hold values from -1 to 1
Outputs:
- msa_out: float32 [64, 64, 256], P(None, 'dap')
- pair_out: float32 [64, 64, 128], P('dap')
All inputs are finite; a program needn't handle non-finite values.
Results may differ from a plain program's by a relative error of at most 0.015.
Values may be sent and summed in bfloat16 or wider, within the bound.
No kernel may reach another device: no remote copies, remote signals or barrier semaphores. Data moves between devices by JAX's collectives and lax.ppermute only.
A program may use at most 64 MiB of HBM per device.

v0:
```python
import math
import jax
import jax.numpy as jnp
from jax import lax
from jax.sharding import PartitionSpec as P

FOCUS_NUMBER = 8
PER_FOCUS_WIDTH = 32
TENSOR_HIDDEN = 32
TRI_HID = 128
EPSILON = 1e-05
MASK_PENALTY_SCALE = 1000000000.0


def standardize_features(content_vectors, gain, axis):
    centred = content_vectors - jnp.mean(content_vectors, axis=axis, keepdims=True)
    spread = jnp.mean(centred * centred, axis=axis, keepdims=True)
    return centred * lax.rsqrt(spread + EPSILON) * gain


def triangle(
    pair_now, gain_in, proj_weight, gate_weight, gain_mid, final_weight, amino_presence, incoming
):
    hidden = TRI_HID
    row_count = pair_now.shape[0]
    my_index = lax.axis_index("dap")
    standardized_source = standardize_features(pair_now, gain_in, -1).astype(jnp.bfloat16)
    projected = jnp.einsum(
        "rkd,de->erk", standardized_source, proj_weight, preferred_element_type=jnp.float32
    )
    res_float = amino_presence.astype(jnp.float32)
    own_rows = lax.dynamic_slice_in_dim(res_float, my_index * row_count, row_count)
    pair_mask = own_rows[:, None] * res_float[None, :]
    left_side = (
        jax.nn.sigmoid(projected[hidden : 2 * hidden]) * projected[:hidden] * pair_mask[None]
    ).astype(jnp.bfloat16)
    right_side = (
        jax.nn.sigmoid(projected[3 * hidden :])
        * projected[2 * hidden : 3 * hidden]
        * pair_mask[None]
    ).astype(jnp.bfloat16)
    gating = jax.nn.sigmoid(
        jnp.dot(standardized_source, gate_weight, preferred_element_type=jnp.float32)
    )
    left_chan, right_chan = (
        lax.all_to_all(left_side, "dap", split_axis=0, concat_axis=1, tiled=True),
        lax.all_to_all(right_side, "dap", split_axis=0, concat_axis=1, tiled=True),
    )
    if incoming:
        product = jnp.einsum(
            "cki,ckj->cij", left_chan, right_chan, preferred_element_type=jnp.float32
        )
    else:
        product = jnp.einsum(
            "cik,cjk->cij", left_chan, right_chan, preferred_element_type=jnp.float32
        )
    product = product.astype(jnp.bfloat16)
    returned = lax.all_to_all(product, "dap", split_axis=1, concat_axis=0, tiled=True)
    product_normed = standardize_features(
        returned.astype(jnp.float32), gain_mid[:, None, None], 0
    ).astype(jnp.bfloat16)
    update = jnp.einsum(
        "crj,cd->rjd", product_normed, final_weight, preferred_element_type=jnp.float32
    )
    return pair_now + update * gating


def shards(
    homolog_stack,
    couple_tensor,
    homolog_presence,
    amino_presence,
    horizontal_standard_factor,
    horizontal_asking_matrix,
    horizontal_lookup_triple,
    horizontal_final_matrix,
    couple_offset_factor,
    couple_offset_matrix,
    vertical_standard_factor,
    vertical_asking_matrix,
    vertical_lookup_triple,
    vertical_final_matrix,
    tensor_average_factor,
    tensor_average_mapping,
    tensor_average_final,
    trio_entry_factors,
    trio_flank_mappings,
    trio_final_switches,
    trio_multiplied_factors,
    trio_final_matrices,
):
    nested_function = FOCUS_NUMBER * PER_FOCUS_WIDTH
    scaling = 1.0 / math.sqrt(PER_FOCUS_WIDTH)
    strand_portion = homolog_stack.shape[0]
    amino_total = homolog_stack.shape[1]
    row_count = couple_tensor.shape[0]
    pair_normed = standardize_features(couple_tensor, couple_offset_factor, -1).astype(jnp.bfloat16)
    bias_local = jnp.einsum(
        "rjc,ch->hrj", pair_normed, couple_offset_matrix, preferred_element_type=jnp.float32
    ).astype(jnp.bfloat16)
    standardized_source = standardize_features(
        homolog_stack, horizontal_standard_factor, -1
    ).astype(jnp.bfloat16)
    shaped = (strand_portion, amino_total, FOCUS_NUMBER, PER_FOCUS_WIDTH)
    queries = (
        (
            jnp.dot(
                standardized_source, horizontal_asking_matrix, preferred_element_type=jnp.float32
            )
            * scaling
        )
        .astype(jnp.bfloat16)
        .reshape(shaped)
    )
    others = jnp.dot(
        standardized_source, horizontal_lookup_triple, preferred_element_type=jnp.float32
    )
    keys_all = others[..., :nested_function].astype(jnp.bfloat16).reshape(shaped)
    content_entire = (
        others[..., nested_function : 2 * nested_function].astype(jnp.bfloat16).reshape(shaped)
    )
    sigmoid_switches = jax.nn.sigmoid(others[..., 2 * nested_function :])
    mask_penalty = MASK_PENALTY_SCALE * (homolog_presence.astype(jnp.float32) - 1.0)

    def attend(bias_piece):
        query_rows = bias_piece.shape[1]
        scores = jnp.einsum(
            "sihc,sjhc->shij", queries, keys_all, preferred_element_type=jnp.float32
        )
        scores = scores + bias_piece.astype(jnp.float32)[None] + mask_penalty[:, None, None, :]
        softmax_probabilities = jax.nn.softmax(scores, axis=-1).astype(jnp.bfloat16)
        mixed = jnp.einsum(
            "shij,sjhc->sihc",
            softmax_probabilities,
            content_entire,
            preferred_element_type=jnp.float32,
        )
        return mixed.reshape(strand_portion, query_rows, nested_function)

    bias_whole = lax.all_gather(bias_local, "dap", axis=1, tiled=True)
    block_rows = math.gcd(amino_total, 256)

    def one_block(block_index):
        return attend(bias_whole)

    blocks = lax.map(one_block, jnp.arange(amino_total // block_rows, dtype=jnp.int32))
    focused_content = jnp.moveaxis(blocks, 0, 1).reshape(
        strand_portion, amino_total, nested_function
    )
    homolog_stack_horizontal = homolog_stack + jnp.dot(
        (focused_content * sigmoid_switches).astype(jnp.bfloat16),
        horizontal_final_matrix,
        preferred_element_type=jnp.float32,
    )
    column_view, col_mask = (
        lax.all_to_all(
            homolog_stack_horizontal.astype(jnp.bfloat16),
            "dap",
            split_axis=1,
            concat_axis=0,
            tiled=True,
        ).astype(homolog_stack_horizontal.dtype),
        lax.all_to_all(
            homolog_presence.astype(jnp.float32).astype(jnp.bfloat16),
            "dap",
            split_axis=1,
            concat_axis=0,
            tiled=True,
        ).astype(jnp.float32),
    )
    seq_total = column_view.shape[0]
    col_shape = (seq_total, row_count, FOCUS_NUMBER, PER_FOCUS_WIDTH)
    standardized_source = standardize_features(column_view, vertical_standard_factor, -1).astype(
        jnp.bfloat16
    )
    col_queries = (
        (
            jnp.dot(standardized_source, vertical_asking_matrix, preferred_element_type=jnp.float32)
            * scaling
        )
        .astype(jnp.bfloat16)
        .reshape(col_shape)
    )
    col_others = jnp.dot(
        standardized_source, vertical_lookup_triple, preferred_element_type=jnp.float32
    )
    col_keys = col_others[..., :nested_function].astype(jnp.bfloat16).reshape(col_shape)
    col_values = (
        col_others[..., nested_function : 2 * nested_function]
        .astype(jnp.bfloat16)
        .reshape(col_shape)
    )
    col_gates = jax.nn.sigmoid(col_others[..., 2 * nested_function :])
    col_penalty = MASK_PENALTY_SCALE * (col_mask - 1.0)
    scores = jnp.einsum(
        "sihc,tihc->ihst", col_queries, col_keys, preferred_element_type=jnp.float32
    )
    scores = scores + jnp.transpose(col_penalty)[:, None, None, :]
    softmax_probabilities = jax.nn.softmax(scores, axis=-1).astype(jnp.bfloat16)
    col_mixed = jnp.einsum(
        "uovg,guox->vuox", softmax_probabilities, col_values, preferred_element_type=jnp.float32
    ).reshape(seq_total, row_count, nested_function)
    alignment_after_columns = column_view + jnp.dot(
        (col_mixed * col_gates).astype(jnp.bfloat16),
        vertical_final_matrix,
        preferred_element_type=jnp.float32,
    )
    standardized_source = standardize_features(
        alignment_after_columns, tensor_average_factor, -1
    ).astype(jnp.bfloat16)
    halves = jnp.dot(
        standardized_source, tensor_average_mapping, preferred_element_type=jnp.float32
    )
    left_proj = (halves[..., :TENSOR_HIDDEN] * col_mask[..., None]).astype(jnp.bfloat16)
    right_proj = (halves[..., TENSOR_HIDDEN:] * col_mask[..., None]).astype(jnp.bfloat16)
    right_whole, mask_whole = (
        lax.all_gather(right_proj, "dap", axis=1, tiled=True),
        lax.all_gather(col_mask.astype(jnp.bfloat16), "dap", axis=1, tiled=True),
    )
    outer = jnp.einsum("sra,sjb->rjab", left_proj, right_whole, preferred_element_type=jnp.float32)
    outer = outer.astype(jnp.bfloat16).reshape(
        row_count, amino_total, TENSOR_HIDDEN * TENSOR_HIDDEN
    )
    counts = jnp.dot(
        jnp.transpose(col_mask), mask_whole.astype(jnp.float32), precision=lax.Precision.HIGHEST
    )
    product = (
        jnp.dot(outer, tensor_average_final, preferred_element_type=jnp.float32)
        / jnp.maximum(counts, 1.0)[..., None]
    )
    pair_one = couple_tensor + product
    pair_two = triangle(
        pair_one,
        trio_entry_factors[0],
        trio_flank_mappings[0],
        trio_final_switches[0],
        trio_multiplied_factors[0],
        trio_final_matrices[0],
        amino_presence,
        False,
    )
    pair_after_incoming = triangle(
        pair_two,
        trio_entry_factors[1],
        trio_flank_mappings[1],
        trio_final_switches[1],
        trio_multiplied_factors[1],
        trio_final_matrices[1],
        amino_presence,
        True,
    )
    return (alignment_after_columns, pair_after_incoming)


def solution(mesh):
    placed = (
        P("dap", None, None),
        P("dap", None, None),
        P("dap", None),
        P(),
        P(),
        P(),
        P(),
        P(),
        P(),
        P(),
        P(),
        P(),
        P(),
        P(),
        P(),
        P(),
        P(),
        P(),
        P(),
        P(),
        P(),
        P(),
    )
    return jax.shard_map(
        shards,
        mesh=mesh,
        in_specs=placed,
        out_specs=(P(None, "dap", None), P("dap", None, None)),
        check_vma=False,
    )
```

profile of v0, /device:TPU:0, one launch (start us, length us, event | category | flops | bytes accessed | tf_op | source)
XLA Modules:
  0.0 221.2 jit_solution(10079408757036569126)
XLA Ops:
  0.7 0.8 convert_convert_fusion
  1.5 0.6 copy.137
  2.2 7.3 %all-to-all-start.1 = ((bf16[2,32,2]{2,0,1:T(2,128)(2,1)}), bf16[2,32,2]{2,0,1:T(2,128)(2,1)S(1)}, u32[]{:S(2)}, u32[]{:S(2)}) async-start(bf16[2,32,2]{2,0,1:T(2,128)(2,1)} %copy.137), calls=%async_computation.1 | async-start | bytes 32768 | tf_op jit(solution)/shard_map/all_to_all | solution.py:163
  9.5 0.7 add_multiply_fusion
  10.2 1.0 reduce_sum.163
  11.4 0.7 copy-done.10
  12.5 0.8 copy-done.6
  13.6 0.7 copy-done.2
  14.6 0.5 copy-done.18
  15.5 42.1 %all_gather.9 = bf16[8,64,64]{2,0,1:T(8,128)(2,1)S(1)} all-gather(bf16[8,2,64]{2,0,1:T(8,128)(2,1)S(1)} %fusion.22), channel_id=1, replica_groups=mesh['dap'=32] {'dap'}, dimensions={1}, use_global_device_ids=true | all-gather | bytes 67584 | tf_op jit(solution)/shard_map/all_gather | solution.py:140
  58.0 0.4 fusion.118
  58.9 0.5 copy-done.13
  59.5 0.7 copy-done.20
  60.5 0.7 copy.126
  61.2 2.6 %all-to-all-start = ((bf16[2,64,256]{2,0,1:T(2,128)(2,1)}), bf16[2,64,256]{2,0,1:T(2,128)(2,1)S(1)}, u32[]{:S(2)}, u32[]{:S(2)}) async-start(bf16[2,64,256]{2,0,1:T(2,128)(2,1)} %copy.126), calls=%async_computation | async-start | bytes 131072 | tf_op jit(solution)/shard_map/all_to_all | solution.py:156
  63.8 41.8 %all-gather = bf16[32,2,64]{2,1,0:T(2,128)(2,1)S(1)} all-gather(bf16[1,2,64]{2,1,0:T(2,128)(2,1)S(1)} %bitcast.220), channel_id=1, replica_groups=mesh['dap'=32] {'dap'}, dimensions={0}, use_global_device_ids=true | all-gather | bytes 8448 | tf_op jit(solution)/shard_map/all_gather | solution.py:218
  107.3 0.6 copy-done.11
  108.3 0.8 copy-done.7
  109.7 0.4 fusion.120
  110.6 0.8 copy-done.16
  111.9 0.6 copy-done.9
  112.8 38.1 %all_gather.10 = bf16[64,64,32]{0,2,1:T(8,128)(2,1)S(1)} all-gather(bf16[64,2,32]{0,2,1:T(8,128)(2,1)S(1)} %fusion.80), channel_id=1, replica_groups=mesh['dap'=32] {'dap'}, dimensions={1}, use_global_device_ids=true | all-gather | bytes 270336 | tf_op jit(solution)/shard_map/all_gather | solution.py:217
  150.9 0.6 fusion.6
  151.9 0.6 copy-done.4
  152.5 0.4 fusion.122
  153.0 0.4 copy-done.5
  153.9 0.7 reshape.256
  154.6 2.6 %all-to-all-start.2 = ((bf16[32,2,256]{2,1,0:T(2,128)(2,1)}), bf16[32,2,256]{2,1,0:T(2,128)(2,1)S(1)}, u32[]{:S(2)}, u32[]{:S(2)}) async-start(bf16[32,2,256]{2,1,0:T(2,128)(2,1)} %reshape.256), calls=%async_computation.2 | async-start | bytes 65536 | tf_op jit(solution)/shard_map/all_to_all | solution.py:46
  157.3 0.7 reshape.258
  158.0 6.4 %all-to-all-done.2 = bf16[32,2,256]{2,1,0:T(2,128)(2,1)S(1)} async-done(((bf16[32,2,256]{2,1,0:T(2,128)(2,1)}), bf16[32,2,256]{2,1,0:T(2,128)(2,1)S(1)}, u32[]{:S(2)}, u32[]{:S(2)}) %all-to-all-start.2) | async-done | bytes 32800 | tf_op jit(solution)/shard_map/all_to_all | solution.py:46
  164.4 2.6 %all-to-all-start.3 = ((bf16[32,2,256]{2,1,0:T(2,128)(2,1)}), bf16[32,2,256]{2,1,0:T(2,128)(2,1)S(1)}, u32[]{:S(2)}, u32[]{:S(2)}) async-start(bf16[32,2,256]{2,1,0:T(2,128)(2,1)} %reshape.258), calls=%async_computation.3 | async-start | bytes 65536 | tf_op jit(solution)/shard_map/all_to_all | solution.py:47
  167.2 7.0 %all-to-all-done.3 = bf16[32,2,256]{2,1,0:T(2,128)(2,1)S(1)} async-done(((bf16[32,2,256]{2,1,0:T(2,128)(2,1)}), bf16[32,2,256]{2,1,0:T(2,128)(2,1)S(1)}, u32[]{:S(2)}, u32[]{:S(2)}) %all-to-all-start.3) | async-done | bytes 32800 | tf_op jit(solution)/shard_map/all_to_all | solution.py:47
  174.7 0.7 reshape.260
  175.4 2.7 %all-to-all-start.4 = ((bf16[32,2,256]{2,1,0:T(2,128)(2,1)}), bf16[32,2,256]{2,1,0:T(2,128)(2,1)S(1)}, u32[]{:S(2)}, u32[]{:S(2)}) async-start(bf16[32,2,256]{2,1,0:T(2,128)(2,1)} %reshape.260), calls=%async_computation.4 | async-start | bytes 65536 | tf_op jit(solution)/shard_map/all_to_all | solution.py:58
  178.2 7.1 %all-to-all-done.4 = bf16[32,2,256]{2,1,0:T(2,128)(2,1)S(1)} async-done(((bf16[32,2,256]{2,1,0:T(2,128)(2,1)}), bf16[32,2,256]{2,1,0:T(2,128)(2,1)S(1)}, u32[]{:S(2)}, u32[]{:S(2)}) %all-to-all-start.4) | async-done | bytes 32800 | tf_op jit(solution)/shard_map/all_to_all | solution.py:58
  185.8 0.7 copy-done.8
  186.7 0.7 copy-done.17
  188.3 0.7 reshape.262
  189.0 2.6 %all-to-all-start.5 = ((bf16[32,2,256]{2,1,0:T(2,128)(2,1)}), bf16[32,2,256]{2,1,0:T(2,128)(2,1)S(1)}, u32[]{:S(2)}, u32[]{:S(2)}) async-start(bf16[32,2,256]{2,1,0:T(2,128)(2,1)} %reshape.262), calls=%async_computation.5 | async-start | bytes 65536 | tf_op jit(solution)/shard_map/all_to_all | solution.py:46
  191.7 0.7 reshape.264
  192.5 6.4 %all-to-all-done.5 = bf16[32,2,256]{2,1,0:T(2,128)(2,1)S(1)} async-done(((bf16[32,2,256]{2,1,0:T(2,128)(2,1)}), bf16[32,2,256]{2,1,0:T(2,128)(2,1)S(1)}, u32[]{:S(2)}, u32[]{:S(2)}) %all-to-all-start.5) | async-done | bytes 32800 | tf_op jit(solution)/shard_map/all_to_all | solution.py:46
  198.9 2.6 %all-to-all-start.6 = ((bf16[32,2,256]{2,1,0:T(2,128)(2,1)}), bf16[32,2,256]{2,1,0:T(2,128)(2,1)S(1)}, u32[]{:S(2)}, u32[]{:S(2)}) async-start(bf16[32,2,256]{2,1,0:T(2,128)(2,1)} %reshape.264), calls=%async_computation.6 | async-start | bytes 65536 | tf_op jit(solution)/shard_map/all_to_all | solution.py:47
  201.6 7.0 %all-to-all-done.6 = bf16[32,2,256]{2,1,0:T(2,128)(2,1)S(1)} async-done(((bf16[32,2,256]{2,1,0:T(2,128)(2,1)}), bf16[32,2,256]{2,1,0:T(2,128)(2,1)S(1)}, u32[]{:S(2)}, u32[]{:S(2)}) %all-to-all-start.6) | async-done | bytes 32800 | tf_op jit(solution)/shard_map/all_to_all | solution.py:47
  209.2 0.7 reshape.266
  209.9 2.6 %all-to-all-start.7 = ((bf16[32,2,256]{2,1,0:T(2,128)(2,1)}), bf16[32,2,256]{2,1,0:T(2,128)(2,1)S(1)}, u32[]{:S(2)}, u32[]{:S(2)}) async-start(bf16[32,2,256]{2,1,0:T(2,128)(2,1)} %reshape.266), calls=%async_computation.7 | async-start | bytes 65536 | tf_op jit(solution)/shard_map/all_to_all | solution.py:58
  212.6 0.8 copy.163
  213.3 6.4 %all-to-all-done.7 = bf16[32,2,256]{2,1,0:T(2,128)(2,1)S(1)} async-done(((bf16[32,2,256]{2,1,0:T(2,128)(2,1)}), bf16[32,2,256]{2,1,0:T(2,128)(2,1)S(1)}, u32[]{:S(2)}, u32[]{:S(2)}) %all-to-all-start.7) | async-done | bytes 32800 | tf_op jit(solution)/shard_map/all_to_all | solution.py:58
  220.3 0.9 fusion.15
  (135 shorter events, 11.6 us)
Async XLA Ops:
  0.6 10.8 %copy-start = (bf16[256,768]{1,0:T(8,128)(2,1)S(1)}, bf16[256,768]{1,0:T(8,128)(2,1)}, u32[]{:S(2)}) copy-start(bf16[256,768]{1,0:T(8,128)(2,1)} %param.28) | copy-start | bytes 1179652
  0.6 10.5 %copy-start.1 = (f32[2,64,256]{2,1,0:T(8,128)S(1)}, f32[2,64,256]{2,1,0:T(8,128)}, u32[]{:S(2)}) copy-start(f32[2,64,256]{2,1,0:T(8,128)} %param.22) | copy-start | bytes 393220
  2.2 59.0 %all-to-all-start.1 = ((bf16[2,32,2]{2,0,1:T(2,128)(2,1)}), bf16[2,32,2]{2,0,1:T(2,128)(2,1)S(1)}, u32[]{:S(2)}, u32[]{:S(2)}) async-start(bf16[2,32,2]{2,0,1:T(2,128)(2,1)} %copy.137), calls=%async_computation.1 | async-start | bytes 32768 | tf_op jit(solution)/shard_map/all_to_all | solution.py:163
  11.4 0.7 copy-start.10
  12.3 0.9 copy-start.6
  13.5 0.8 copy-start.2
  14.4 0.7 copy-start.18
  14.6 0.7 copy-start.19
  58.8 0.7 copy-start.13
  58.8 1.4 copy-start.15
  59.5 0.7 copy-start.20
  61.2 44.6 %all-to-all-start = ((bf16[2,64,256]{2,0,1:T(2,128)(2,1)}), bf16[2,64,256]{2,0,1:T(2,128)(2,1)S(1)}, u32[]{:S(2)}, u32[]{:S(2)}) async-start(bf16[2,64,256]{2,0,1:T(2,128)(2,1)} %copy.126), calls=%async_computation | async-start | bytes 131072 | tf_op jit(solution)/shard_map/all_to_all | solution.py:156
  106.3 1.0 copy-start.3
  107.2 0.7 copy-start.11
  108.2 0.9 copy-start.7
  110.5 0.9 copy-start.16
  111.7 0.8 copy-start.9
  111.9 0.7 copy-start.12
  151.5 1.0 copy-start.4
  152.5 0.9 copy-start.5
  154.6 9.8 %all-to-all-start.2 = ((bf16[32,2,256]{2,1,0:T(2,128)(2,1)}), bf16[32,2,256]{2,1,0:T(2,128)(2,1)S(1)}, u32[]{:S(2)}, u32[]{:S(2)}) async-start(bf16[32,2,256]{2,1,0:T(2,128)(2,1)} %reshape.256), calls=%async_computation.2 | async-start | bytes 65536 | tf_op jit(solution)/shard_map/all_to_all | solution.py:46
  164.4 9.8 %all-to-all-start.3 = ((bf16[32,2,256]{2,1,0:T(2,128)(2,1)}), bf16[32,2,256]{2,1,0:T(2,128)(2,1)S(1)}, u32[]{:S(2)}, u32[]{:S(2)}) async-start(bf16[32,2,256]{2,1,0:T(2,128)(2,1)} %reshape.258), calls=%async_computation.3 | async-start | bytes 65536 | tf_op jit(solution)/shard_map/all_to_all | solution.py:47
  175.4 2.7 %copy-start.14 = (f32[2,128]{1,0:T(2,128)S(1)}, f32[2,128]{1,0:T(2,128)}, u32[]{:S(2)}) copy-start(f32[2,128]{1,0:T(2,128)} %param.42) | copy-start | bytes 3076
  175.4 10.0 %all-to-all-start.4 = ((bf16[32,2,256]{2,1,0:T(2,128)(2,1)}), bf16[32,2,256]{2,1,0:T(2,128)(2,1)S(1)}, u32[]{:S(2)}, u32[]{:S(2)}) async-start(bf16[32,2,256]{2,1,0:T(2,128)(2,1)} %reshape.260), calls=%async_computation.4 | async-start | bytes 65536 | tf_op jit(solution)/shard_map/all_to_all | solution.py:58
  185.6 0.8 copy-start.8
  186.5 0.8 copy-start.17
  189.0 9.8 %all-to-all-start.5 = ((bf16[32,2,256]{2,1,0:T(2,128)(2,1)}), bf16[32,2,256]{2,1,0:T(2,128)(2,1)S(1)}, u32[]{:S(2)}, u32[]{:S(2)}) async-start(bf16[32,2,256]{2,1,0:T(2,128)(2,1)} %reshape.262), calls=%async_computation.5 | async-start | bytes 65536 | tf_op jit(solution)/shard_map/all_to_all | solution.py:46
  198.9 9.8 %all-to-all-start.6 = ((bf16[32,2,256]{2,1,0:T(2,128)(2,1)}), bf16[32,2,256]{2,1,0:T(2,128)(2,1)S(1)}, u32[]{:S(2)}, u32[]{:S(2)}) async-start(bf16[32,2,256]{2,1,0:T(2,128)(2,1)} %reshape.264), calls=%async_computation.6 | async-start | bytes 65536 | tf_op jit(solution)/shard_map/all_to_all | solution.py:47
  209.9 9.8 %all-to-all-start.7 = ((bf16[32,2,256]{2,1,0:T(2,128)(2,1)}), bf16[32,2,256]{2,1,0:T(2,128)(2,1)S(1)}, u32[]{:S(2)}, u32[]{:S(2)}) async-start(bf16[32,2,256]{2,1,0:T(2,128)(2,1)} %reshape.266), calls=%async_computation.7 | async-start | bytes 65536 | tf_op jit(solution)/shard_map/all_to_all | solution.py:58
where the time goes:
time: 222 us; the launch traced here: 221 us
  blocking collectives  122 us (55%)
  waiting for transfers between devices  40.4 us (18%)
  starting transfers between devices  25.4 us (11%)
  local copies, waits for them, and re-layouts  20.1 us (9%)
  matrix products  7.19 us (3%)
  other arithmetic  4.68 us (2%)
    all_gather x1, blocking collectives, shards(): bias_whole = lax.all_gather(bias_local, 'dap', axis=1, tiled=True)  42.1 us
    all_gather x1, blocking collectives, shards(): lax.all_gather(col_mask.astype(jnp.bfloat16), 'dap', axis=1, tiled=True)  41.8 us
    all_gather x1, blocking collectives, shards(): lax.all_gather(right_proj, 'dap', axis=1, tiled=True)  38.1 us
    unnamed x55, local copies, waits for them, and re-layouts  15 us
    all_to_all x2, waiting for transfers between devices, triangle(): lax.all_to_all(right_side, 'dap', split_axis=0, concat_axis=1, tiled=True)  14.1 us
    all_to_all x2, waiting for transfers between devices, triangle(): lax.all_to_all(product, 'dap', split_axis=1, concat_axis=0, tiled=True)  13.5 us
    all_to_all x2, waiting for transfers between devices, triangle(): lax.all_to_all(left_side, 'dap', split_axis=0, concat_axis=1, tiled=True)  12.8 us
    all_to_all x1, starting transfers between devices, shards(): lax.all_to_all(homolog_presence.astype(jnp.float32).astype(jnp.bfloat16),...  7.33 us
  transfers between devices with their start and end apart: 8, of which 6 were waited for; matrix products, arithmetic and copies ran while one was open for 4% of the time, Pallas kernels for 0%

commit v1 on v0

--- a/solution.py
+++ b/solution.py
@@ -3,6 +3,7 @@
 import jax.numpy as jnp
 from jax import lax
 from jax.sharding import PartitionSpec as P
+from jax.lax import all_to_all, axis_size
 
 FOCUS_NUMBER = 8
 PER_FOCUS_WIDTH = 32
@@ -213,9 +214,25 @@
     )
     left_proj = (halves[..., :TENSOR_HIDDEN] * col_mask[..., None]).astype(jnp.bfloat16)
     right_proj = (halves[..., TENSOR_HIDDEN:] * col_mask[..., None]).astype(jnp.bfloat16)
+
+    def detail_the_stocks(buf, comm_axis, dim_i):
+        series = []
+        h = 0
+        axis_total = axis_size(comm_axis)
+        while h < buf.ndim:
+            series.append(axis_total if h == dim_i else 1)
+            h += 1
+        return all_to_all(
+            jnp.tile(buf, series),
+            axis_name=comm_axis,
+            split_axis=dim_i,
+            concat_axis=dim_i,
+            tiled=True,
+        )
+
     right_whole, mask_whole = (
         lax.all_gather(right_proj, "dap", axis=1, tiled=True),
-        lax.all_gather(col_mask.astype(jnp.bfloat16), "dap", axis=1, tiled=True),
+        detail_the_stocks(col_mask.astype(jnp.bfloat16), "dap", 1),
     )
     outer = jnp.einsum("sra,sjb->rjab", left_proj, right_whole, preferred_element_type=jnp.float32)
     outer = outer.astype(jnp.bfloat16).reshape(

time: 222 us -> 198 us (0.89)
  blocking collectives: 122 us -> 80.7 us
  waiting for transfers between devices: 40.4 us -> 54.7 us
  starting transfers between devices: 25.4 us -> 28 us
    all_gather x1 -> x0, blocking collectives: 41.8 us -> none  [shards(): lax.all_gather(col_mask.astype(jnp.bfloat16), 'dap', axis=1, tiled=True)]
    all_to_all x1, waiting for transfers between devices: 0.01 us -> 7.23 us  [shards(): lax.all_to_all(homolog_stack_horizontal.astype(jnp.bfloat16), 'dap', spli...]
    all_to_all x0 -> x1, waiting for transfers between devices: none -> 7.08 us  [detail_the_stocks(): all_to_all(jnp.tile(buf, series), axis_name=comm_axis, split_axis=dim_i,...]
    all_to_all x0 -> x1, starting transfers between devices: none -> 2.54 us  [detail_the_stocks(): all_to_all(jnp.tile(buf, series), axis_name=comm_axis, split_axis=dim_i,...]
  transfers between devices with their start and end apart: 8 -> 9, of which waited for: 6 -> 8; matrix products, arithmetic and copies ran while one was open for 4% -> 4% of each run, Pallas kernels for 0% -> 0%
where the time goes in v1:
time: 198 us; the launch traced here: 197 us
  blocking collectives  80.7 us (41%)
  waiting for transfers between devices  54.7 us (28%)
  starting transfers between devices  28 us (14%)
  local copies, waits for them, and re-layouts  20.8 us (11%)
  matrix products  7.2 us (4%)
  other arithmetic  4.67 us (2%)
    all_gather x1, blocking collectives, shards(): bias_whole = lax.all_gather(bias_local, 'dap', axis=1, tiled=True)  42.1 us
    all_gather x1, blocking collectives, shards(): lax.all_gather(right_proj, 'dap', axis=1, tiled=True)  38.6 us
    unnamed x55, local copies, waits for them, and re-layouts  15 us
    all_to_all x2, waiting for transfers between devices, triangle(): lax.all_to_all(right_side, 'dap', split_axis=0, concat_axis=1, tiled=True)  14.1 us
    all_to_all x2, waiting for transfers between devices, triangle(): lax.all_to_all(product, 'dap', split_axis=1, concat_axis=0, tiled=True)  13.5 us
    all_to_all x2, waiting for transfers between devices, triangle(): lax.all_to_all(left_side, 'dap', split_axis=0, concat_axis=1, tiled=True)  12.8 us
    all_to_all x1, starting transfers between devices, shards(): lax.all_to_all(homolog_presence.astype(jnp.float32).astype(jnp.bfloat16),...  7.33 us
    all_to_all x1, waiting for transfers between devices, shards(): lax.all_to_all(homolog_stack_horizontal.astype(jnp.bfloat16), 'dap', spli...  7.23 us
  transfers between devices with their start and end apart: 9, of which 8 were waited for; matrix products, arithmetic and copies ran while one was open for 4% of the time, Pallas kernels for 0%

profile of v1, /device:TPU:0, one launch (start us, length us, event | category | flops | bytes accessed | tf_op | source)
XLA Modules:
  0.0 197.4 jit_solution(9561489988238035967)
XLA Ops:
  0.7 0.8 convert_convert_fusion
  1.5 0.6 copy.138
  2.2 7.3 %all-to-all-start.1 = ((bf16[2,32,2]{2,0,1:T(2,128)(2,1)}), bf16[2,32,2]{2,0,1:T(2,128)(2,1)S(1)}, u32[]{:S(2)}, u32[]{:S(2)}) async-start(bf16[2,32,2]{2,0,1:T(2,128)(2,1)} %copy.138), calls=%async_computation.1 | async-start | bytes 32768 | tf_op jit(solution)/shard_map/all_to_all | solution.py:164
  9.5 0.7 add_multiply_fusion
  10.2 1.0 reduce_sum.163
  11.4 0.7 copy-done.10
  12.5 0.8 copy-done.6
  13.6 0.7 copy-done.2
  14.6 0.5 copy-done.18
  15.5 42.1 %all_gather.6 = bf16[8,64,64]{2,0,1:T(8,128)(2,1)S(1)} all-gather(bf16[8,2,64]{2,0,1:T(8,128)(2,1)S(1)} %fusion.22), channel_id=1, replica_groups=mesh['dap'=32] {'dap'}, dimensions={1}, use_global_device_ids=true | all-gather | bytes 67584 | tf_op jit(solution)/shard_map/all_gather | solution.py:141
  58.0 0.4 fusion.118
  58.9 0.5 copy-done.13
  59.5 0.7 copy-done.20
  60.5 0.7 copy.127
  61.2 0.6 tile.2
  61.9 2.5 %all-to-all-start.2 = ((bf16[64,32,2]{0,2,1:T(2,128)(2,1)}), bf16[64,32,2]{0,2,1:T(2,128)(2,1)S(1)}, u32[]{:S(2)}, u32[]{:S(2)}) async-start(bf16[64,32,2]{0,2,1:T(2,128)(2,1)} %tile.2), calls=%async_computation.2 | async-start | bytes 32768 | tf_op jit(solution)/shard_map/all_to_all | solution.py:225
  64.5 7.1 %all-to-all-done.2 = bf16[64,32,2]{0,2,1:T(2,128)(2,1)S(1)} async-done(((bf16[64,32,2]{0,2,1:T(2,128)(2,1)}), bf16[64,32,2]{0,2,1:T(2,128)(2,1)S(1)}, u32[]{:S(2)}, u32[]{:S(2)}) %all-to-all-start.2) | async-done | bytes 8224 | tf_op jit(solution)/shard_map/all_to_all | solution.py:225
  71.5 2.6 %all-to-all-start = ((bf16[2,64,256]{2,0,1:T(2,128)(2,1)}), bf16[2,64,256]{2,0,1:T(2,128)(2,1)S(1)}, u32[]{:S(2)}, u32[]{:S(2)}) async-start(bf16[2,64,256]{2,0,1:T(2,128)(2,1)} %copy.127), calls=%async_computation | async-start | bytes 131072 | tf_op jit(solution)/shard_map/all_to_all | solution.py:157
  74.3 7.2 %all-to-all-done = bf16[2,64,256]{2,0,1:T(2,128)(2,1)S(1)} async-done(((bf16[2,64,256]{2,0,1:T(2,128)(2,1)}), bf16[2,64,256]{2,0,1:T(2,128)(2,1)S(1)}, u32[]{:S(2)}, u32[]{:S(2)}) %all-to-all-start) | async-done | bytes 65568 | tf_op jit(solution)/shard_map/all_to_all | solution.py:157
  83.0 0.6 copy-done.11
  84.0 0.8 copy-done.7
  86.3 0.8 copy-done.16
  87.6 0.6 copy-done.9
  88.5 38.6 %all_gather.7 = bf16[64,64,32]{0,2,1:T(8,128)(2,1)S(1)} all-gather(bf16[64,2,32]{0,2,1:T(8,128)(2,1)S(1)} %fusion.80), channel_id=1, replica_groups=mesh['dap'=32] {'dap'}, dimensions={1}, use_global_device_ids=true | all-gather | bytes 270336 | tf_op jit(solution)/shard_map/all_gather | solution.py:234
  127.1 0.6 fusion.6
  128.1 0.6 copy-done.4
  130.1 0.7 reshape.262
  130.9 2.6 %all-to-all-start.3 = ((bf16[32,2,256]{2,1,0:T(2,128)(2,1)}), bf16[32,2,256]{2,1,0:T(2,128)(2,1)S(1)}, u32[]{:S(2)}, u32[]{:S(2)}) async-start(bf16[32,2,256]{2,1,0:T(2,128)(2,1)} %reshape.262), calls=%async_computation.3 | async-start | bytes 65536 | tf_op jit(solution)/shard_map/all_to_all | solution.py:47
  133.6 0.7 reshape.264
  134.3 6.4 %all-to-all-done.3 = bf16[32,2,256]{2,1,0:T(2,128)(2,1)S(1)} async-done(((bf16[32,2,256]{2,1,0:T(2,128)(2,1)}), bf16[32,2,256]{2,1,0:T(2,128)(2,1)S(1)}, u32[]{:S(2)}, u32[]{:S(2)}) %all-to-all-start.3) | async-done | bytes 32800 | tf_op jit(solution)/shard_map/all_to_all | solution.py:47
  140.7 2.6 %all-to-all-start.4 = ((bf16[32,2,256]{2,1,0:T(2,128)(2,1)}), bf16[32,2,256]{2,1,0:T(2,128)(2,1)S(1)}, u32[]{:S(2)}, u32[]{:S(2)}) async-start(bf16[32,2,256]{2,1,0:T(2,128)(2,1)} %reshape.264), calls=%async_computation.4 | async-start | bytes 65536 | tf_op jit(solution)/shard_map/all_to_all | solution.py:48
  143.5 7.0 %all-to-all-done.4 = bf16[32,2,256]{2,1,0:T(2,128)(2,1)S(1)} async-done(((bf16[32,2,256]{2,1,0:T(2,128)(2,1)}), bf16[32,2,256]{2,1,0:T(2,128)(2,1)S(1)}, u32[]{:S(2)}, u32[]{:S(2)}) %all-to-all-start.4) | async-done | bytes 32800 | tf_op jit(solution)/shard_map/all_to_all | solution.py:48
  151.0 0.7 reshape.266
  151.7 2.7 %all-to-all-start.5 = ((bf16[32,2,256]{2,1,0:T(2,128)(2,1)}), bf16[32,2,256]{2,1,0:T(2,128)(2,1)S(1)}, u32[]{:S(2)}, u32[]{:S(2)}) async-start(bf16[32,2,256]{2,1,0:T(2,128)(2,1)} %reshape.266), calls=%async_computation.5 | async-start | bytes 65536 | tf_op jit(solution)/shard_map/all_to_all | solution.py:59
  154.5 7.1 %all-to-all-done.5 = bf16[32,2,256]{2,1,0:T(2,128)(2,1)S(1)} async-done(((bf16[32,2,256]{2,1,0:T(2,128)(2,1)}), bf16[32,2,256]{2,1,0:T(2,128)(2,1)S(1)}, u32[]{:S(2)}, u32[]{:S(2)}) %all-to-all-start.5) | async-done | bytes 32800 | tf_op jit(solution)/shard_map/all_to_all | solution.py:59
  162.0 0.7 copy-done.8
  162.9 0.7 copy-done.17
  164.6 0.7 reshape.268
  165.3 2.6 %all-to-all-start.6 = ((bf16[32,2,256]{2,1,0:T(2,128)(2,1)}), bf16[32,2,256]{2,1,0:T(2,128)(2,1)S(1)}, u32[]{:S(2)}, u32[]{:S(2)}) async-start(bf16[32,2,256]{2,1,0:T(2,128)(2,1)} %reshape.268), calls=%async_computation.6 | async-start | bytes 65536 | tf_op jit(solution)/shard_map/all_to_all | solution.py:47
  168.0 0.7 reshape.270
  168.7 6.4 %all-to-all-done.6 = bf16[32,2,256]{2,1,0:T(2,128)(2,1)S(1)} async-done(((bf16[32,2,256]{2,1,0:T(2,128)(2,1)}), bf16[32,2,256]{2,1,0:T(2,128)(2,1)S(1)}, u32[]{:S(2)}, u32[]{:S(2)}) %all-to-all-start.6) | async-done | bytes 32800 | tf_op jit(solution)/shard_map/all_to_all | solution.py:47
  175.1 2.6 %all-to-all-start.7 = ((bf16[32,2,256]{2,1,0:T(2,128)(2,1)}), bf16[32,2,256]{2,1,0:T(2,128)(2,1)S(1)}, u32[]{:S(2)}, u32[]{:S(2)}) async-start(bf16[32,2,256]{2,1,0:T(2,128)(2,1)} %reshape.270), calls=%async_computation.7 | async-start | bytes 65536 | tf_op jit(solution)/shard_map/all_to_all | solution.py:48
  177.9 7.0 %all-to-all-done.7 = bf16[32,2,256]{2,1,0:T(2,128)(2,1)S(1)} async-done(((bf16[32,2,256]{2,1,0:T(2,128)(2,1)}), bf16[32,2,256]{2,1,0:T(2,128)(2,1)S(1)}, u32[]{:S(2)}, u32[]{:S(2)}) %all-to-all-start.7) | async-done | bytes 32800 | tf_op jit(solution)/shard_map/all_to_all | solution.py:48
  185.4 0.7 reshape.272
  186.2 2.6 %all-to-all-start.8 = ((bf16[32,2,256]{2,1,0:T(2,128)(2,1)}), bf16[32,2,256]{2,1,0:T(2,128)(2,1)S(1)}, u32[]{:S(2)}, u32[]{:S(2)}) async-start(bf16[32,2,256]{2,1,0:T(2,128)(2,1)} %reshape.272), calls=%async_computation.8 | async-start | bytes 65536 | tf_op jit(solution)/shard_map/all_to_all | solution.py:59
  188.9 0.8 copy.164
  189.6 6.4 %all-to-all-done.8 = bf16[32,2,256]{2,1,0:T(2,128)(2,1)S(1)} async-done(((bf16[32,2,256]{2,1,0:T(2,128)(2,1)}), bf16[32,2,256]{2,1,0:T(2,128)(2,1)S(1)}, u32[]{:S(2)}, u32[]{:S(2)}) %all-to-all-start.8) | async-done | bytes 32800 | tf_op jit(solution)/shard_map/all_to_all | solution.py:59
  196.6 0.9 fusion.15
  (137 shorter events, 12.7 us)
Async XLA Ops:
  0.6 10.8 %copy-start = (bf16[256,768]{1,0:T(8,128)(2,1)S(1)}, bf16[256,768]{1,0:T(8,128)(2,1)}, u32[]{:S(2)}) copy-start(bf16[256,768]{1,0:T(8,128)(2,1)} %param.28) | copy-start | bytes 1179652
  0.6 10.5 %copy-start.1 = (f32[2,64,256]{2,1,0:T(8,128)S(1)}, f32[2,64,256]{2,1,0:T(8,128)}, u32[]{:S(2)}) copy-start(f32[2,64,256]{2,1,0:T(8,128)} %param.22) | copy-start | bytes 393220
  2.2 59.0 %all-to-all-start.1 = ((bf16[2,32,2]{2,0,1:T(2,128)(2,1)}), bf16[2,32,2]{2,0,1:T(2,128)(2,1)S(1)}, u32[]{:S(2)}, u32[]{:S(2)}) async-start(bf16[2,32,2]{2,0,1:T(2,128)(2,1)} %copy.138), calls=%async_computation.1 | async-start | bytes 32768 | tf_op jit(solution)/shard_map/all_to_all | solution.py:164
  11.4 0.7 copy-start.10
  12.3 0.9 copy-start.6
  13.5 0.8 copy-start.2
  14.4 0.7 copy-start.18
  14.6 0.7 copy-start.19
  58.8 0.7 copy-start.13
  58.8 1.4 copy-start.15
  59.5 0.7 copy-start.20
  61.9 9.7 %all-to-all-start.2 = ((bf16[64,32,2]{0,2,1:T(2,128)(2,1)}), bf16[64,32,2]{0,2,1:T(2,128)(2,1)S(1)}, u32[]{:S(2)}, u32[]{:S(2)}) async-start(bf16[64,32,2]{0,2,1:T(2,128)(2,1)} %tile.2), calls=%async_computation.2 | async-start | bytes 32768 | tf_op jit(solution)/shard_map/all_to_all | solution.py:225
  71.5 10.0 %all-to-all-start = ((bf16[2,64,256]{2,0,1:T(2,128)(2,1)}), bf16[2,64,256]{2,0,1:T(2,128)(2,1)S(1)}, u32[]{:S(2)}, u32[]{:S(2)}) async-start(bf16[2,64,256]{2,0,1:T(2,128)(2,1)} %copy.127), calls=%async_computation | async-start | bytes 131072 | tf_op jit(solution)/shard_map/all_to_all | solution.py:157
  82.0 1.0 copy-start.3
  82.9 0.7 copy-start.11
  83.9 0.9 copy-start.7
  86.2 0.9 copy-start.16
  87.4 0.8 copy-start.9
  87.6 0.7 copy-start.12
  127.8 1.0 copy-start.4
  128.7 0.9 copy-start.5
  130.9 9.8 %all-to-all-start.3 = ((bf16[32,2,256]{2,1,0:T(2,128)(2,1)}), bf16[32,2,256]{2,1,0:T(2,128)(2,1)S(1)}, u32[]{:S(2)}, u32[]{:S(2)}) async-start(bf16[32,2,256]{2,1,0:T(2,128)(2,1)} %reshape.262), calls=%async_computation.3 | async-start | bytes 65536 | tf_op jit(solution)/shard_map/all_to_all | solution.py:47
  140.7 9.8 %all-to-all-start.4 = ((bf16[32,2,256]{2,1,0:T(2,128)(2,1)}), bf16[32,2,256]{2,1,0:T(2,128)(2,1)S(1)}, u32[]{:S(2)}, u32[]{:S(2)}) async-start(bf16[32,2,256]{2,1,0:T(2,128)(2,1)} %reshape.264), calls=%async_computation.4 | async-start | bytes 65536 | tf_op jit(solution)/shard_map/all_to_all | solution.py:48
  151.7 2.7 %copy-start.14 = (f32[2,128]{1,0:T(2,128)S(1)}, f32[2,128]{1,0:T(2,128)}, u32[]{:S(2)}) copy-start(f32[2,128]{1,0:T(2,128)} %param.42) | copy-start | bytes 3076
  151.7 10.0 %all-to-all-start.5 = ((bf16[32,2,256]{2,1,0:T(2,128)(2,1)}), bf16[32,2,256]{2,1,0:T(2,128)(2,1)S(1)}, u32[]{:S(2)}, u32[]{:S(2)}) async-start(bf16[32,2,256]{2,1,0:T(2,128)(2,1)} %reshape.266), calls=%async_computation.5 | async-start | bytes 65536 | tf_op jit(solution)/shard_map/all_to_all | solution.py:59
  161.9 0.8 copy-start.8
  162.8 0.8 copy-start.17
  165.3 9.8 %all-to-all-start.6 = ((bf16[32,2,256]{2,1,0:T(2,128)(2,1)}), bf16[32,2,256]{2,1,0:T(2,128)(2,1)S(1)}, u32[]{:S(2)}, u32[]{:S(2)}) async-start(bf16[32,2,256]{2,1,0:T(2,128)(2,1)} %reshape.268), calls=%async_computation.6 | async-start | bytes 65536 | tf_op jit(solution)/shard_map/all_to_all | solution.py:47
  175.1 9.8 %all-to-all-start.7 = ((bf16[32,2,256]{2,1,0:T(2,128)(2,1)}), bf16[32,2,256]{2,1,0:T(2,128)(2,1)S(1)}, u32[]{:S(2)}, u32[]{:S(2)}) async-start(bf16[32,2,256]{2,1,0:T(2,128)(2,1)} %reshape.270), calls=%async_computation.7 | async-start | bytes 65536 | tf_op jit(solution)/shard_map/all_to_all | solution.py:48
  186.2 9.8 %all-to-all-start.8 = ((bf16[32,2,256]{2,1,0:T(2,128)(2,1)}), bf16[32,2,256]{2,1,0:T(2,128)(2,1)S(1)}, u32[]{:S(2)}, u32[]{:S(2)}) async-start(bf16[32,2,256]{2,1,0:T(2,128)(2,1)} %reshape.272), calls=%async_computation.8 | async-start | bytes 65536 | tf_op jit(solution)/shard_map/all_to_all | solution.py:59
